TPU v7x, 32 devices: a whole 2x2x4 slice. The times are simulated.
32 devices in a mesh: section: 2 (over x), dp: 4 (over z), mp: 4 (over y, core).
Axes of the slice: x: 2, y: 2, z: 4, core: 2. Of those that a mesh axis runs over, the one named last changes fastest.
Arguments:
- hidden: bfloat16 [2, 512, 4096], P('section', 'dp'), may hold values from -9 to 9
- norm_gain: float32 [2, 4096], P('section'), may hold values from 0.5 to 1.5
- kv_weight: bfloat16 [2, 4096, 2048], P('section', None, 'mp'), may hold values from -1 to 1
- attn_flat: bfloat16 [2, 4, 8388608], P('section', 'mp', 'dp'), may hold values from -1 to 1
- final_gain: float32 [4096], replicated, may hold values from 0.5 to 1.5
- reward_head: float32 [4096], replicated, may hold values from -0.09375 to 0.09375
- segment_ids: int32 [2, 4], P('section'), may hold values from 0 to 2, never falling along the last dimension, each value on 1 to 2 neighbouring positions
- ranks: int32 [2], replicated, may hold values from 0 to 999
Outputs:
- next_hidden: bfloat16 [2, 512, 4096], P('section', 'dp')
- rewards: float32 [2], replicated
- pair_loss: float32 [2, 2], replicated
Inputs may be any that keep to these rules, and one draw needn't show every extreme that they name: `segment_ids`: each row's segment numbers never fall, every number of 0 to 2 is present, each on 1 to 2 blocks, one on exactly 2.
All inputs are finite; a program needn't handle non-finite values.
Results may differ from a plain program's by a relative error of at most 0.035.
Values may be sent and summed in bfloat16 or wider, within the bound.
A program may use at most 128 MiB of HBM per device.

v0:
```python
import jax
import jax.numpy as jnp
from jax import lax
from jax.sharding import PartitionSpec as P

HD = 128
QH = 32
KVH = 8
EPS = 1e-05


def passed_along(block, axis, distance):
    devices = range(lax.axis_size(axis))
    route = [(i - distance, i) for i in devices if i - distance in devices]
    return lax.ppermute(block, axis, route)


def shards(hidden, norm_gain, kv_weight, attn_flat, final_gain, reward_head, segment_ids, ranks):
    state = hidden[0]
    tokens = state.shape[0]
    width = state.shape[1]
    seg_row = segment_ids[0]
    blocks = lax.axis_size("dp")
    block = lax.axis_index("dp")
    phases = lax.axis_size("section")
    phase_now = lax.axis_index("section")
    responses = ranks.shape[0]
    state_wide = state.astype(jnp.float32)
    normed = (
        state_wide
        * lax.rsqrt(jnp.mean(state_wide * state_wide, -1, keepdims=True) + EPS)
        * norm_gain[0]
    ).astype(jnp.bfloat16)
    keyval = jnp.dot(normed, kv_weight[0], preferred_element_type=jnp.float32).astype(jnp.bfloat16)
    kv_local = keyval.shape[1] // (2 * HD)
    group = QH // KVH
    q_width = kv_local * group * HD
    flat = lax.all_gather(attn_flat[0, 0], "dp", axis=0, tiled=True)
    w_query = flat[: width * q_width].reshape(width, q_width)
    w_out = flat[width * q_width : 2 * width * q_width].reshape(q_width, width)
    query = jnp.dot(normed, w_query, preferred_element_type=jnp.float32).astype(jnp.bfloat16)
    query = query.reshape(tokens, kv_local, group, HD)
    block_ids = jnp.arange(blocks, dtype=jnp.int32)
    own_seg = jnp.sum(jnp.where(block_ids == block, seg_row, 0))
    query_pos = block * tokens + jnp.arange(tokens, dtype=jnp.int32)
    piece = lax.all_gather(keyval, "dp", axis=0, tiled=True)
    peak = jnp.full((kv_local, group, tokens), -1e30, jnp.float32)
    count = piece.shape[0]
    key_pos = jnp.arange(count, dtype=jnp.int32)
    key_block = key_pos // tokens
    key_seg = jnp.sum(jnp.where(key_block[:, None] == block_ids[None, :], seg_row[None, :], 0), 1)
    parts = piece.reshape(count, kv_local, 2, HD)
    keys = parts[:, :, 0]
    values = parts[:, :, 1]
    earlier = (key_block < block) & (key_block >= 0) & ((key_seg == 0) | (key_seg == own_seg))
    same = (key_block == block)[None, :] & (key_pos[None, :] <= query_pos[:, None])
    visible = earlier[None, :] | same
    scores = jnp.einsum("tjgd,cjd->jgtc", query, keys, preferred_element_type=jnp.float32) * HD ** (
        -0.5
    )
    scores = jnp.where(visible[None, None], scores, -1e30)
    new_peak = jnp.maximum(peak, jnp.max(scores, -1))
    weights = jnp.where(visible[None, None], jnp.exp(scores - new_peak[..., None]), 0.0)
    total = jnp.sum(weights, -1)
    accum = jnp.einsum(
        "jgtc,cjd->jgtd", weights.astype(jnp.bfloat16), values, preferred_element_type=jnp.float32
    )
    peak, total, accum = (new_peak, total, accum)
    mixed = (
        (accum / total[..., None])
        .transpose(2, 0, 1, 3)
        .reshape(tokens, q_width)
        .astype(jnp.bfloat16)
    )
    partial_value = jnp.dot(mixed, w_out, preferred_element_type=jnp.float32)
    ends = (
        jnp.sum(
            (seg_row[None, :] <= jnp.arange(1, responses + 1, dtype=jnp.int32)[:, None]).astype(
                jnp.int32
            ),
            1,
        )
        - 1
    )
    at_end = (ends == block) & (phase_now == phases - 1)
    summed = lax.psum(partial_value.astype(jnp.bfloat16), "mp").astype(jnp.float32)
    updated = (state_wide + summed).astype(jnp.bfloat16)
    moved = passed_along(updated, "section", 1)
    last_row = updated[tokens - 1].astype(jnp.float32)
    squares = jnp.sum(last_row * last_row)
    product = jnp.sum(last_row * final_gain * reward_head)
    sums_sq, dots = lax.psum(
        (jnp.where(at_end, squares, 0.0), jnp.where(at_end, product, 0.0)), ("section", "dp")
    )
    rewards = dots * lax.rsqrt(sums_sq / width + EPS)
    pair_loss = jnp.where(
        ranks[:, None] < ranks[None, :], jax.nn.softplus(rewards[None, :] - rewards[:, None]), 0.0
    )
    return (moved[None], rewards, pair_loss)


def solution(mesh):
    placed = (
        P("section", "dp", None),
        P("section", None),
        P("section", None, "mp"),
        P("section", "mp", "dp"),
        P(),
        P(),
        P("section", None),
        P(),
    )
    return jax.shard_map(
        shards,
        mesh=mesh,
        in_specs=placed,
        out_specs=(P("section", "dp", None), P(), P()),
        check_vma=False,
    )
```

profile of v0, /device:TPU:0, one launch (start us, length us, event | category | flops | bytes accessed | tf_op | source)
XLA Modules:
  0.0 864.1 jit_solution(7415746184136145379)
XLA Ops:
  7.2 0.0 copy-start.1
  7.2 0.0 copy-start.7
  7.2 0.0 all-gather.3.cloned.1.call-start
  7.2 0.7 all-gather.3.cloned.1.call-update
  7.9 0.0 all-reduce.3.cloned.1.call-start
  8.0 0.4 copy-done.1
  8.4 0.3 fusion.5
  8.7 0.0 copy-done.7
  8.7 2.9 fusion.16
  11.6 17.4 %all_gather.6 = bf16[512,512]{1,0:T(8,128)(2,1)S(1)} all-gather(bf16[128,512]{1,0:T(8,128)(2,1)S(1)} %fusion.16), channel_id=1, replica_groups=mesh['section'=2,'dp'=4,'mp'=4] {'dp'}, dimensions={0}, use_global_device_ids=true | all-gather | bytes 655360 | tf_op jit(solution)/shard_map/all_gather | solution.py:46
  29.0 0.0 copy-start.6
  29.0 0.1 reshape.161
  29.1 0.7 fusion.48
  29.9 0.7 copy.22
  30.6 0.0 copy-done.6
  30.6 0.6 fusion.44
  31.2 0.1 select_reduce_fusion
  31.3 0.7 or_and_fusion
  32.0 0.2 fusion.35
  32.2 541.5 %all-gather.3.cloned.1.call-done = bf16[1,1,8388608]{2,1,0:T(2,128)(2,1)} async-done(((bf16[1,1,2097152]{2,1,0:T(2,128)(2,1)}), bf16[1,1,8388608]{2,1,0:T(2,128)(2,1)}) %all-gather.3.cloned.1.call-update) | async-done | bytes 16777232 | tf_op jit(solution)/shard_map/all_gather | solution.py:38
  573.7 183.8 %slice_reduce_fusion = (bf16[4194304]{0:T(1024)(128)(2,1)}, bf16[4194304]{0:T(1024)(128)(2,1)}) fusion(bf16[1,1,8388608]{2,1,0:T(2,128)(2,1)} %all-gather.3.cloned.1.call-done), kind=kLoop, calls=%fused_computation | loop fusion | bytes 33554432 | tf_op jit(solution)/shard_map/slice | solution.py:40
  757.6 13.3 %slice.40 = bf16[1024,4096]{1,0:T(8,128)(2,1)} reshape(bf16[4194304]{0:T(1024)(128)(2,1)} %get-tuple-element.3) | data formatting | bytes 16777216 | tf_op jit(solution)/shard_map/slice | solution.py:40
  770.9 13.3 %slice.37 = bf16[4096,1024]{1,0:T(8,128)(2,1)} reshape(bf16[4194304]{0:T(1024)(128)(2,1)} %get-tuple-element.4) | data formatting | bytes 16777216 | tf_op jit(solution)/shard_map/slice | solution.py:39
  784.2 4.7 convolution_convert_fusion.1
  788.9 0.2 reshape.162
  789.0 0.0 copy-start
  789.0 0.5 fusion.11
  789.5 0.5 fusion.12
  790.1 0.7 fusion.15
  790.7 1.7 copy-done
  792.4 2.3 convolution_convert_fusion
  794.7 0.0 copy-start.2
  794.7 0.0 copy-start.3
  794.7 0.0 copy-start.4
  794.7 0.0 all-reduce.3.cloned.1.call-update
  794.7 0.2 fusion.43
  794.9 34.2 %all-reduce.3.cloned.1.call-done = bf16[128,4096]{1,0:T(8,128)(2,1)} async-done(((bf16[128,4096]{1,0:T(8,128)(2,1)}), bf16[128,4096]{1,0:T(8,128)(2,1)}) %all-reduce.3.cloned.1.call-update) | async-done | bytes 1048592 | tf_op jit(solution)/shard_map/psum | solution.py:86
  829.1 1.5 fusion.8
  830.6 3.4 collective-permute-start
  834.1 0.0 copy-done.2
  834.1 0.0 copy-done.3
  834.1 0.6 multiply_reduce_fusion
  834.7 1.3 broadcast_select_fusion
  836.0 19.5 %all-reduce = (f32[2]{0:T(128)S(1)}, f32[2]{0:T(128)S(1)}) all-reduce(f32[2]{0:T(128)S(1)} %get-tuple-element.12, f32[2]{0:T(128)S(1)} %get-tuple-element.11), channel_id=1, replica_groups=mesh['section'=2,'dp'=4,'mp'=4] {'section','dp'}, use_global_device_ids=true, to_apply=%region_8.9 | all-reduce | flops 4 | bytes 32 | tf_op jit(solution)/shard_map/psum | solution.py:92
  855.5 0.0 copy-done.4
  855.5 0.0 copy-start.5
  855.5 0.7 compare_select_fusion.1
  856.2 0.1 collective-permute-done
  856.3 1.0 copy.34
  857.3 0.0 copy-done.5
  (7 shorter events, 0.0 us)
Async XLA Ops:
  7.2 1.2 copy-start.1
  7.2 1.5 copy-start.7
  7.2 566.5 %all-gather.3.cloned.1.call-start = ((), (), s32[]{:S(2)}) async-start(), calls=%async_computation.1 | async-start | bytes 41943040 | tf_op jit(solution)/shard_map/all_gather | solution.py:38
  7.9 821.2 %all-reduce.3.cloned.1.call-start = ((), (), s32[]{:S(2)}) async-start(), calls=%async_computation | async-start | bytes 2097152 | tf_op jit(solution)/shard_map/psum | solution.py:86
  29.0 1.6 copy-start.6
  789.0 3.4 copy-start
  794.7 39.4 %copy-start.2 = (f32[4096]{0:T(1024)S(1)}, f32[4096]{0:T(1024)}, u32[]{:S(2)}) copy-start(f32[4096]{0:T(1024)} %param.13) | copy-start | bytes 49156
  794.7 39.4 %copy-start.3 = (f32[4096]{0:T(1024)S(1)}, f32[4096]{0:T(1024)}, u32[]{:S(2)}) copy-start(f32[4096]{0:T(1024)} %param.12) | copy-start | bytes 49156
  794.7 60.9 %copy-start.4 = (s32[2]{0:T(128)S(1)}, s32[2]{0:T(128)}, u32[]{:S(2)}) copy-start(s32[2]{0:T(128)} %param.15) | copy-start | bytes 28
  830.6 25.7 %collective-permute-start = (bf16[128,4096]{1,0:T(8,128)(2,1)S(1)}, bf16[128,4096]{1,0:T(8,128)(2,1)S(1)}, u32[]{:S(2)}, u32[]{:S(2)}) collective-permute-start(bf16[128,4096]{1,0:T(8,128)(2,1)S(1)} %fusion.8), channel_id=1, source_target_pairs={{0,16},{1,17},{2,18},{3,19},{4,20},{5,21},{6,22},{7,23},{8,24},{9,... | collective-permute-start | bytes 3145736 | tf_op jit(solution)/shard_map/ppermute | solution.py:15
  855.5 1.8 copy-start.5
Sparse Core Ops, SparseCore 0:
  9.6 564.0 all-gather.2
  794.8 34.2 all-reduce.2
where the time goes:
time: 865 us; the launch traced here: 864 us
  waiting for transfers between devices  577 us (67%)
  local copies, waits for them, and re-layouts  215 us (25%)
  blocking collectives  36.9 us (4%)
  between operations  14.3 us (2%)
  matrix products  11 us (1%)
    all_gather x1, waiting for transfers between devices, shards(): flat = lax.all_gather(attn_flat[0, 0], 'dp', axis=0, tiled=True)  542 us
    slice x2, local copies, waits for them, and re-layouts, shards(): w_out = flat[width * q_width:2 * width * q_width].reshape(q_width, width)  197 us
    psum x1, waiting for transfers between devices, shards(): lax.psum(partial_value.astype(jnp.bfloat16), 'mp').astype(jnp.float32)  34.2 us
    psum x1, blocking collectives, shards(): lax.psum((jnp.where(at_end, squares, 0.0), jnp.where(at_end, product, 0.0...  19.5 us
    all_gather x1, blocking collectives, shards(): piece = lax.all_gather(keyval, 'dp', axis=0, tiled=True)  17.4 us
  transfers between devices with their start and end apart: 3, of which 3 were waited for; matrix products, arithmetic and copies ran while one was open for 1% of the time, Pallas kernels for 0%

commit v1 on v0

--- a/solution.py
+++ b/solution.py
@@ -7,6 +7,11 @@
 QH = 32
 KVH = 8
 EPS = 1e-05
+
+
+def extend_steps_all_by_axis(vector):
+    response = lax.psum(vector, axis_name="dp")
+    return lax.psum(response, axis_name="section")
 
 
 def passed_along(block, axis, distance):
@@ -89,8 +94,8 @@
     last_row = updated[tokens - 1].astype(jnp.float32)
     squares = jnp.sum(last_row * last_row)
     product = jnp.sum(last_row * final_gain * reward_head)
-    sums_sq, dots = lax.psum(
-        (jnp.where(at_end, squares, 0.0), jnp.where(at_end, product, 0.0)), ("section", "dp")
+    sums_sq, dots = extend_steps_all_by_axis(
+        (jnp.where(at_end, squares, 0.0), jnp.where(at_end, product, 0.0))
     )
     rewards = dots * lax.rsqrt(sums_sq / width + EPS)
     pair_loss = jnp.where(

time: 865 us -> 866 us (level)
    psum x1 -> x2, blocking collectives: 19.5 us -> 20 us  [the longest x1 11.7 us: extend_steps_all_by_axis(): response = lax.psum(vector, axis_name='dp')]
  transfers between devices with their start and end apart: 3 -> 3, of which waited for: 3 -> 2; matrix products, arithmetic and copies ran while one was open for 1% -> 1% of each run, Pallas kernels for 0% -> 0%
where the time goes in v1:
time: 866 us; the launch traced here: 865 us
  waiting for transfers between devices  576 us (67%)
  local copies, waits for them, and re-layouts  215 us (25%)
  blocking collectives  37.4 us (4%)
  between operations  14.2 us (2%)
  matrix products  11 us (1%)
    all_gather x1, waiting for transfers between devices, shards(): flat = lax.all_gather(attn_flat[0, 0], 'dp', axis=0, tiled=True)  542 us
    slice x2, local copies, waits for them, and re-layouts, shards(): w_out = flat[width * q_width:2 * width * q_width].reshape(q_width, width)  197 us
    psum x1, waiting for transfers between devices, shards(): lax.psum(partial_value.astype(jnp.bfloat16), 'mp').astype(jnp.float32)  34.2 us
    all_gather x1, blocking collectives, shards(): piece = lax.all_gather(keyval, 'dp', axis=0, tiled=True)  17.4 us
  transfers between devices with their start and end apart: 3, of which 2 were waited for; matrix products, arithmetic and copies ran while one was open for 1% of the time, Pallas kernels for 0%

profile of v1, /device:TPU:0, one launch (start us, length us, event | category | flops | bytes accessed | tf_op | source)
XLA Modules:
  0.0 864.5 jit_solution(10173166650345601188)
XLA Ops:
  7.2 0.0 copy-start.1
  7.2 0.0 copy-start.7
  7.2 0.0 all-gather.3.cloned.1.call-start
  7.2 0.7 all-gather.3.cloned.1.call-update
  7.9 0.0 all-reduce.4.cloned.1.call-start
  8.0 0.4 copy-done.1
  8.4 0.3 fusion.5
  8.7 0.0 copy-done.7
  8.7 2.9 fusion.16
  11.6 17.4 %all_gather.6 = bf16[512,512]{1,0:T(8,128)(2,1)S(1)} all-gather(bf16[128,512]{1,0:T(8,128)(2,1)S(1)} %fusion.16), channel_id=1, replica_groups=mesh['section'=2,'dp'=4,'mp'=4] {'dp'}, dimensions={0}, use_global_device_ids=true | all-gather | bytes 655360 | tf_op jit(solution)/shard_map/all_gather | solution.py:51
  29.0 0.0 copy-start.6
  29.0 0.1 reshape.161
  29.1 0.7 fusion.48
  29.9 0.7 copy.22
  30.6 0.0 copy-done.6
  30.6 0.6 fusion.44
  31.2 0.1 select_reduce_fusion
  31.3 0.7 or_and_fusion
  32.0 0.2 fusion.35
  32.2 541.5 %all-gather.3.cloned.1.call-done = bf16[1,1,8388608]{2,1,0:T(2,128)(2,1)} async-done(((bf16[1,1,2097152]{2,1,0:T(2,128)(2,1)}), bf16[1,1,8388608]{2,1,0:T(2,128)(2,1)}) %all-gather.3.cloned.1.call-update) | async-done | bytes 16777232 | tf_op jit(solution)/shard_map/all_gather | solution.py:43
  573.7 183.8 %slice_reduce_fusion = (bf16[4194304]{0:T(1024)(128)(2,1)}, bf16[4194304]{0:T(1024)(128)(2,1)}) fusion(bf16[1,1,8388608]{2,1,0:T(2,128)(2,1)} %all-gather.3.cloned.1.call-done), kind=kLoop, calls=%fused_computation | loop fusion | bytes 33554432 | tf_op jit(solution)/shard_map/slice | solution.py:45
  757.6 13.3 %slice.40 = bf16[1024,4096]{1,0:T(8,128)(2,1)} reshape(bf16[4194304]{0:T(1024)(128)(2,1)} %get-tuple-element.3) | data formatting | bytes 16777216 | tf_op jit(solution)/shard_map/slice | solution.py:45
  770.9 13.3 %slice.37 = bf16[4096,1024]{1,0:T(8,128)(2,1)} reshape(bf16[4194304]{0:T(1024)(128)(2,1)} %get-tuple-element.4) | data formatting | bytes 16777216 | tf_op jit(solution)/shard_map/slice | solution.py:44
  784.2 4.7 convolution_convert_fusion.1
  788.9 0.2 reshape.162
  789.0 0.0 copy-start
  789.0 0.5 fusion.11
  789.5 0.5 fusion.12
  790.1 0.7 fusion.15
  790.7 1.7 copy-done
  792.4 2.3 convolution_convert_fusion
  794.7 0.0 copy-start.2
  794.7 0.0 copy-start.3
  794.7 0.0 copy-start.4
  794.7 0.0 all-reduce.4.cloned.1.call-update
  794.7 0.2 fusion.43
  794.9 34.2 %all-reduce.4.cloned.1.call-done = bf16[128,4096]{1,0:T(8,128)(2,1)} async-done(((bf16[128,4096]{1,0:T(8,128)(2,1)}), bf16[128,4096]{1,0:T(8,128)(2,1)}) %all-reduce.4.cloned.1.call-update) | async-done | bytes 1048592 | tf_op jit(solution)/shard_map/psum | solution.py:91
  829.1 1.5 fusion.8
  830.6 3.4 collective-permute-start
  834.1 0.0 copy-done.2
  834.1 0.0 copy-done.3
  834.1 0.6 multiply_reduce_fusion
  834.7 1.3 broadcast_select_fusion
  836.0 11.7 %all-reduce = (f32[2]{0:T(128)S(1)}, f32[2]{0:T(128)S(1)}) all-reduce(f32[2]{0:T(128)S(1)} %get-tuple-element.14, f32[2]{0:T(128)S(1)} %get-tuple-element.13), channel_id=1, replica_groups=mesh['section'=2,'dp'=4,'mp'=4] {'dp'}, use_global_device_ids=true, to_apply=%region_8.9 | all-reduce | flops 4 | bytes 32 | tf_op jit(solution)/shard_map/psum | solution.py:13
  847.7 8.3 all-reduce.1
  856.1 0.0 copy-done.4
  856.1 0.0 copy-start.5
  856.1 0.7 compare_select_fusion.1
  856.7 0.0 collective-permute-done
  856.7 1.0 copy.34
  857.7 0.0 copy-done.5
  (7 shorter events, 0.0 us)
Async XLA Ops:
  7.2 1.2 copy-start.1
  7.2 1.5 copy-start.7
  7.2 566.5 %all-gather.3.cloned.1.call-start = ((), (), s32[]{:S(2)}) async-start(), calls=%async_computation.1 | async-start | bytes 41943040 | tf_op jit(solution)/shard_map/all_gather | solution.py:43
  7.9 821.2 %all-reduce.4.cloned.1.call-start = ((), (), s32[]{:S(2)}) async-start(), calls=%async_computation | async-start | bytes 2097152 | tf_op jit(solution)/shard_map/psum | solution.py:91
  29.0 1.6 copy-start.6
  789.0 3.4 copy-start
  794.7 39.4 %copy-start.2 = (f32[4096]{0:T(1024)S(1)}, f32[4096]{0:T(1024)}, u32[]{:S(2)}) copy-start(f32[4096]{0:T(1024)} %param.13) | copy-start | bytes 49156
  794.7 39.4 %copy-start.3 = (f32[4096]{0:T(1024)S(1)}, f32[4096]{0:T(1024)}, u32[]{:S(2)}) copy-start(f32[4096]{0:T(1024)} %param.12) | copy-start | bytes 49156
  794.7 61.4 %copy-start.4 = (s32[2]{0:T(128)S(1)}, s32[2]{0:T(128)}, u32[]{:S(2)}) copy-start(s32[2]{0:T(128)} %param.15) | copy-start | bytes 28
  830.6 26.1 %collective-permute-start = (bf16[128,4096]{1,0:T(8,128)(2,1)S(1)}, bf16[128,4096]{1,0:T(8,128)(2,1)S(1)}, u32[]{:S(2)}, u32[]{:S(2)}) collective-permute-start(bf16[128,4096]{1,0:T(8,128)(2,1)S(1)} %fusion.8), channel_id=1, source_target_pairs={{0,16},{1,17},{2,18},{3,19},{4,20},{5,21},{6,22},{7,23},{8,24},{9,... | collective-permute-start | bytes 3145736 | tf_op jit(solution)/shard_map/ppermute | solution.py:20
  856.1 1.6 copy-start.5
Sparse Core Ops, SparseCore 0:
  9.6 564.0 all-gather.2
  794.8 34.2 all-reduce.3
